TPU v7x, 32 devices: a whole 2x2x4 slice. The times are simulated.
32 devices in a mesh: member: 2 (over y), tile: 4 (over z), chan: 2 (over x), sub: 2 (over core).
Axes of the slice: x: 2, y: 2, z: 4, core: 2. Of those that a mesh axis runs over, the one named last changes fastest.
Arguments:
- obs_values: bfloat16 [131072, 64], P(('member', 'tile', 'chan', 'sub')), parts along dimension 0, may hold values from -6 to 6
- obs_weight: bfloat16 [131072], P(('member', 'tile', 'chan', 'sub')), parts along dimension 0, may hold values from 0.25 to 4
- obs_tile: int32 [131072], P(('member', 'tile', 'chan', 'sub')), parts along dimension 0, may hold values from 0 to 7, as said below
- obs_cell: int32 [131072], P(('member', 'tile', 'chan', 'sub')), parts along dimension 0, may hold values from 0 to 3071
- conv_one: bfloat16 [3, 3, 256, 64], P(None, None, 'chan'), may hold values from -0.25 to 0.25
- conv_two: bfloat16 [3, 3, 256, 256], P(None, None, 'chan'), may hold values from -0.125 to 0.125
- density_gain: float32 [256], P('chan'), may hold values from -2 to 2
- cotangent: bfloat16 [512, 32, 768], P(('member', 'chan'), 'tile', 'sub'), parts along dimension 0, may hold values from -6 to 6
Outputs:
- encoded: bfloat16 [512, 32, 768], P(('member', 'chan'), 'tile', 'sub'), parts along dimension 0
- grad_conv_one: float32 [6, 3, 256, 64], P('member', None, 'chan'), parts along dimension 0
- grad_conv_two: float32 [6, 3, 256, 256], P('member', None, 'chan'), parts along dimension 0
- grad_gain: float32 [512], P(('member', 'chan')), parts along dimension 0
There are 2 independent parts, one for each index of `member`. A program takes and returns all parts, laid end to end along the dimension named above; an argument that names none is the same for every part. Nothing has to cross between parts.
Inputs may be any that keep to these rules, and one draw needn't show every extreme that they name: `obs_tile`: among the rows of one device no tile is named by more than 1024 rows, and one tile, the same for every device of a member, is named by exactly 1024 of them.
All inputs are finite; a program needn't handle non-finite values.
Results may differ from a plain program's by a relative error of at most 0.0055.
Values may be sent and summed in bfloat16 or wider, within the bound.
No kernel may reach another device: no remote copies, remote signals or barrier semaphores. Data moves between devices by JAX's collectives and lax.ppermute only.
A program may use at most 64 MiB of HBM per device.

v0:
```python
import math
import jax
import jax.numpy as jnp
from jax import lax
from jax.sharding import PartitionSpec as P


def padded_2(block, sides, width):
    for axis, dim in sides:
        count = lax.axis_size(axis)
        forward = [(i, i + 1) for i in range(count - 1)]
        backward = [(target, source) for source, target in forward]
        low = lax.ppermute(
            lax.slice_in_dim(block, block.shape[dim] - width, None, axis=dim), axis, forward
        )
        high = lax.ppermute(lax.slice_in_dim(block, 0, width, axis=dim), axis, backward)
        block = jnp.concatenate([low, block, high], axis=dim)
    return block


def conv_apply(padded, kernel):
    n_rows = padded.shape[1] - 2
    n_cols = padded.shape[2] - 2
    summed = None
    for row_off in range(3):
        for col_off in range(3):
            window = padded[:, row_off : row_off + n_rows, col_off : col_off + n_cols]
            product_term = jnp.einsum(
                "oc,chw->ohw", kernel[row_off, col_off], window, preferred_element_type=jnp.float32
            )
            summed = product_term if summed is None else summed + product_term
    return summed


def kernel_grad(out_grad, padded):
    n_rows = out_grad.shape[1]
    n_cols = out_grad.shape[2]
    blocks = []
    for row_off in range(3):
        row_terms = []
        for col_off in range(3):
            window = padded[:, row_off : row_off + n_rows, col_off : col_off + n_cols]
            row_terms.append(
                jnp.einsum("ohw,chw->oc", out_grad, window, preferred_element_type=jnp.float32)
            )
        blocks.append(jnp.stack(row_terms))
    return jnp.stack(blocks)


def back_apply(padded_grad, kernel_cols):
    n_rows = padded_grad.shape[1] - 2
    n_cols = padded_grad.shape[2] - 2
    summed = None
    for row_off in range(3):
        for col_off in range(3):
            window = padded_grad[
                :, 2 - row_off : 2 - row_off + n_rows, 2 - col_off : 2 - col_off + n_cols
            ]
            product_term = jnp.einsum(
                "oc,ohw->chw",
                kernel_cols[row_off, col_off],
                window,
                preferred_element_type=jnp.float32,
            )
            summed = product_term if summed is None else summed + product_term
    return summed


def grid_local(flat_values, flat_weight, cell_flat, n_cells):
    n_recv = flat_values.shape[0]
    obs_chans = flat_values.shape[1]
    block_rows = math.gcd(n_recv, 1024)
    n_blocks = n_recv // block_rows
    cell_ids = jnp.arange(n_cells, dtype=jnp.int32)
    ones_col = jnp.ones((block_rows,), jnp.bfloat16)

    def add_block(carry, pieces):
        data_acc, dens_acc = carry
        block_vals, block_weight, block_cell = pieces
        placing = jnp.where(
            block_cell[None, :] == cell_ids[:, None],
            block_weight[None, :],
            jnp.zeros((), jnp.bfloat16),
        )
        data_acc = data_acc + jnp.einsum(
            "ij,ci->jc", block_vals, placing, preferred_element_type=jnp.float32
        )
        dens_acc = dens_acc + jnp.dot(placing, ones_col, preferred_element_type=jnp.float32)
        return ((data_acc, dens_acc), None)

    start = (jnp.zeros((obs_chans, n_cells), jnp.float32), jnp.zeros((n_cells,), jnp.float32))
    (data_acc, dens_acc), unused = lax.scan(
        add_block,
        start,
        (
            flat_values.reshape(n_blocks, block_rows, obs_chans),
            flat_weight.reshape(n_blocks, block_rows),
            cell_flat.reshape(n_blocks, block_rows),
        ),
    )
    return (data_acc, dens_acc)


def body(obs_values, obs_weight, obs_tile, obs_cell, conv_one, conv_two, density_gain, cotangent):
    n_rows = cotangent.shape[1]
    n_cols = cotangent.shape[2]
    n_cells = n_rows * n_cols
    n_tiles = lax.axis_size("tile") * lax.axis_size("sub")
    n_obs = obs_values.shape[0]
    obs_chans = obs_values.shape[1]
    capacity = 2 * n_obs // n_tiles
    onehot = (obs_tile[:, None] == jnp.arange(n_tiles, dtype=jnp.int32)[None, :]).astype(jnp.int32)
    slots = jnp.sum(jnp.cumsum(onehot, axis=0) * onehot, axis=1) - 1
    dest_slot = obs_tile * capacity + slots
    source = (
        jnp.full((n_tiles * capacity,), n_obs, jnp.int32)
        .at[dest_slot]
        .set(jnp.arange(n_obs, dtype=jnp.int32))
    )
    filled = source < n_obs
    pick = jnp.minimum(source, n_obs - 1)
    send_values = jnp.where(
        filled[:, None], jnp.take(obs_values, pick, axis=0), jnp.zeros((), jnp.bfloat16)
    )
    send_values = send_values.reshape(n_tiles, capacity * obs_chans)
    send_weight = jnp.where(
        filled, jnp.take(obs_weight, pick), jnp.zeros((), jnp.bfloat16)
    ).reshape(n_tiles, capacity)
    send_cell = jnp.where(filled, jnp.take(obs_cell, pick), 0).reshape(n_tiles, capacity)
    got_values, got_weight, got_cell = (
        lax.all_to_all(send_values, ("tile", "sub"), split_axis=0, concat_axis=0, tiled=True),
        lax.all_to_all(send_weight, ("tile", "sub"), split_axis=0, concat_axis=0, tiled=True),
        lax.all_to_all(send_cell, ("tile", "sub"), split_axis=0, concat_axis=0, tiled=True),
    )
    flat_values = got_values.reshape(-1, obs_chans)
    flat_weight = got_weight.reshape(-1)
    cell_flat = got_cell.reshape(-1)
    data_grid, dens_grid = grid_local(flat_values, flat_weight, cell_flat, n_cells)
    data_part = data_grid.reshape(obs_chans, n_rows, n_cols)
    dens_part = dens_grid.reshape(n_rows, n_cols)
    data_sum, density = lax.psum((data_part, dens_part), "chan")
    features = (data_sum / (1.0 + density)[None]).astype(jnp.bfloat16)
    log_density = jnp.log1p(density)
    feats_pad = padded_2(features, (("tile", 1), ("sub", 2)), 1)
    pre_one = conv_apply(feats_pad, conv_one) + density_gain[:, None, None] * log_density[None]
    hidden = jax.nn.silu(pre_one).astype(jnp.bfloat16)
    hidden_own = padded_2(hidden, (("tile", 1), ("sub", 2)), 1)
    hidden_pad = lax.all_gather(hidden_own, "chan", axis=0, tiled=True)
    encoded = conv_apply(hidden_pad, conv_two).astype(jnp.bfloat16)
    cot_pad = padded_2(cotangent, (("tile", 1), ("sub", 2)), 1)
    grad_two = kernel_grad(cotangent, hidden_pad)
    cot_full = lax.all_gather(cot_pad, "chan", axis=0, tiled=True)
    kernel_cols = lax.all_to_all(conv_two, "chan", split_axis=3, concat_axis=2, tiled=True)
    grad_hidden = back_apply(cot_full, kernel_cols)
    sigma = jax.nn.sigmoid(pre_one)
    grad_pre = (grad_hidden * sigma * (1.0 + pre_one * (1.0 - sigma))).astype(jnp.bfloat16)
    grad_one = kernel_grad(grad_pre, feats_pad)
    grad_gain = jnp.sum(grad_pre.astype(jnp.float32) * log_density[None], axis=(1, 2))
    summed_one, summed_two, summed_gain = lax.psum((grad_one, grad_two, grad_gain), ("tile", "sub"))
    scale_factor = 1.0 / math.sqrt(n_tiles * n_cells)
    return (
        encoded,
        summed_one * scale_factor,
        summed_two * scale_factor,
        summed_gain * scale_factor,
    )


def solution(mesh):
    placed = (
        P(("member", "tile", "chan", "sub"), None),
        P(("member", "tile", "chan", "sub")),
        P(("member", "tile", "chan", "sub")),
        P(("member", "tile", "chan", "sub")),
        P(None, None, "chan", None),
        P(None, None, "chan", None),
        P("chan"),
        P(("member", "chan"), "tile", "sub"),
    )
    return jax.shard_map(
        body,
        mesh=mesh,
        in_specs=placed,
        out_specs=(
            P(("member", "chan"), "tile", "sub"),
            P("member", None, "chan", None),
            P("member", None, "chan", None),
            P(("member", "chan")),
        ),
        check_vma=False,
    )
```

profile of v0, /device:TPU:0, one launch (start us, length us, event | category | flops | bytes accessed | tf_op | source)
XLA Modules:
  0.0 491.1 jit_solution(184157803824915240)
XLA Ops:
  7.9 2.3 reduce-window.6
  12.4 15.5 %scatter_custom_fusion = s32[8192]{0:T(1024)S(1)} fusion(s32[4096]{0:T(1024)S(1)} %compare_select_fusion.1, s32[4096]{0:T(1024)S(1)} %iota.14, s32[]{:T(128)} %constant.46.clone.1), kind=kCustom, calls=%fused_computation.211 | custom fusion | bytes 32772 | tf_op jit(solution)/shard_map/scatter | solution.py:118
  28.0 50.7 %gather_fusion.2 = bf16[8192]{0:T(1024)(128)(2,1)S(1)} fusion(bf16[4096]{0:T(1024)(128)(2,1)S(1)} %copy-done.2, s32[8192]{0:T(1024)S(1)} %fusion.153), kind=kCustom, calls=%fused_computation.2 | custom fusion | bytes 65536 | tf_op jit(solution)/shard_map/jit(_take)/gather | solution.py:127
  80.7 6.3 %all-to-all-start.2 = ((bf16[8,2,512]{2,1,0:T(2,128)(2,1)}), bf16[8,2,512]{2,1,0:T(2,128)(2,1)S(1)}, u32[]{:S(2)}, u32[]{:S(2)}) async-start(bf16[8,2,512]{2,1,0:T(2,128)(2,1)} %reshape.179), calls=%async_computation.2 | async-start | bytes 32768 | tf_op jit(solution)/shard_map/all_to_all | solution.py:132
  87.0 45.5 %gather_fusion.1 = s32[8192]{0:T(1024)S(1)} fusion(s32[4096]{0:T(1024)S(1)} %copy-done, s32[8192]{0:T(1024)S(1)} %fusion.153), kind=kCustom, calls=%fused_computation.1 | custom fusion | bytes 98304 | tf_op jit(solution)/shard_map/jit(_take)/gather | solution.py:129
  133.2 5.1 %all-to-all-start.1 = ((s32[8,1,1024]{2,1,0:T(1,128)}), s32[8,1,1024]{2,1,0:T(1,128)S(1)}, u32[]{:S(2)}, u32[]{:S(2)}) async-start(s32[8,1,1024]{2,1,0:T(1,128)} %bitcast.2), calls=%async_computation.1 | async-start | bytes 65536 | tf_op jit(solution)/shard_map/all_to_all | solution.py:133
  139.6 2.1 broadcast_in_dim.90
  141.7 2.5 broadcast_in_dim.91
  144.2 2.1 broadcast_in_dim.93
  146.3 2.5 broadcast_in_dim.94
  149.3 24.0 %gather_fusion = bf16[8192,64]{1,0:T(8,128)(2,1)S(1)} fusion(bf16[4096,64]{1,0:T(8,128)(2,1)S(1)} %copy.118, s32[8192]{0:T(1024)S(1)} %fusion.153), kind=kCustom, calls=%fused_computation | custom fusion | bytes 2129920 | tf_op jit(solution)/shard_map/jit(_take)/gather | solution.py:123
  173.3 1.5 gather.15
  174.9 4.4 all-to-all-start.3
  181.0 1.9 reshape.177
  182.9 8.3 %all-to-all-done.3 = bf16[3,3,128,256]{2,1,0,3:T(4,128)(2,1)} async-done(((bf16[3,3,128,256]{2,1,0,3:T(4,128)(2,1)}), bf16[3,3,128,256]{2,1,0,3:T(4,128)(2,1)}, u32[]{:S(2)}, u32[]{:S(2)}) %all-to-all-start.3) | async-done | bytes 589856 | tf_op jit(solution)/shard_map/all_to_all | solution.py:153
  191.2 4.7 all-to-all-start
  196.6 3.9 collective-permute-start.8
  201.9 14.1 %collective-permute-done.8 = bf16[128,1,384]{0,2,1:T(8,128)(2,1)S(1)} collective-permute-done((bf16[128,1,384]{0,2,1:T(8,128)(2,1)S(1)}, bf16[128,1,384]{0,2,1:T(8,128)(2,1)S(1)}, u32[]{:S(2)}, u32[]{:S(2)}) %collective-permute-start.8) | collective-permute-done | bytes 98336 | tf_op jit(solution)/shard_map/ppermute | solution.py:13
  216.0 1.8 collective-permute-start.10
  219.3 1.7 collective-permute-done.11
  222.2 2.2 copy.126
  225.5 6.4 %reduce.2 = bf16[8,65536]{1,0:T(8,128)(2,1)S(1)} reduce(bf16[8,1,65536]{2,1,0:T(2,128)(2,1)S(1)} %reshape.178, bf16[]{:T(256)} %constant.88), dimensions={1}, to_apply=%all_to_all.33.reduce_sub_computation | reduce | bytes 2097154 | tf_op jit(solution)/shard_map/all_to_all | solution.py:131
  231.8 2.2 reshape_reshape.3
  234.1 38.9 %while.13 = (s32[]{:T(128)}, f32[64,3072]{1,0:T(8,128)}, f32[3072]{0:T(1024)S(1)}, bf16[8,1024,64]{2,1,0:T(8,128)(2,1)S(1)}, s32[8,1024]{1,0:T(8,128)S(1)}, /*in...) while((s32[]{:T(128)}, f32[64,3072]{1,0:T(8,128)}, f32[3072]{0:T(1024)S(1)}, ...), condition=%wide.region_5.6_spmd.clone, body=%wide.region_4.5_spmd.clone.sunk | while | flops 421926912 | bytes 8200364 | solution.py:92
  234.1 1.7 fusion.214
  235.9 2.2 fusion.213
  239.0 1.7 fusion.214
  240.8 2.2 fusion.213
  243.9 1.7 fusion.214
  245.6 2.2 fusion.213
  248.7 1.7 fusion.214
  250.5 2.2 fusion.213
  253.6 1.7 fusion.214
  255.3 2.2 fusion.213
  258.5 1.7 fusion.214
  260.2 2.2 fusion.213
  263.3 1.7 fusion.214
  265.1 2.2 fusion.213
  268.2 1.7 fusion.214
  269.9 2.2 fusion.213
  273.0 2.1 copy.182
  275.1 6.9 %psum.36 = f32[8,384]{1,0:T(8,128)S(1)} all-reduce(f32[8,384]{1,0:T(8,128)S(1)} %reshape.88), channel_id=1, replica_groups=mesh['member'=2,'tile'=4,'chan'=2,'sub'=2] {'chan'}, use_global_device_ids=true, to_apply=%region_7.8 | all-reduce | flops 3072 | bytes 24576 | tf_op jit(solution)/shard_map/psum | solution.py:141
  282.4 3.3 fusion.25
  285.7 1.8 fusion.27
  287.4 1.7 fusion.29
  289.2 1.8 fusion.31
  291.0 1.7 fusion.33
  292.7 1.7 fusion.35
  294.4 1.8 fusion.37
  296.2 1.8 fusion.39
  298.0 25.5 %all-reduce.4.cloned.1.call-done = f32[64,8,384]{2,0,1:T(8,128)} async-done(((f32[64,8,384]{2,0,1:T(8,128)}), f32[64,8,384]{2,0,1:T(8,128)}) %all-reduce.4.cloned.1.call-update) | async-done | bytes 786448 | tf_op jit(solution)/shard_map/psum | solution.py:141
  324.7 3.4 collective-permute-start
  329.9 4.3 collective-permute-done.1
  335.5 3.0 collective-permute-start.2
  342.5 1.5 multiply_convert_fusion
  347.3 2.4 multiply_reduce_fusion
  350.4 3.4 collective-permute-start.4
  356.4 4.1 collective-permute-done.5
  363.2 14.7 %psum.39 = f32[128]{0:T(128)S(1)} all-reduce(f32[128]{0:T(128)S(1)} %get-tuple-element.118), channel_id=1, replica_groups=mesh['member'=2,'tile'=4,'chan'=2,'sub'=2] {'tile','sub'}, use_global_device_ids=true, to_apply=%region_11.12 | all-reduce | flops 128 | bytes 1024 | tf_op jit(solution)/shard_map/psum | solution.py:159
  377.9 2.4 pad_maximum_fusion.1
  383.8 25.9 %all-gather.3.cloned.1.call-done = bf16[256,10,386]{0,2,1:T(8,128)(2,1)} async-done(((bf16[128,10,386]{0,2,1:T(8,128)(2,1)}), bf16[256,10,386]{0,2,1:T(8,128)(2,1)}) %all-gather.3.cloned.1.call-update) | async-done | bytes 1976336 | tf_op jit(solution)/shard_map/all_gather | solution.py:148
  409.7 2.4 fusion.101
  425.5 54.1 %all-reduce.6.cloned.1.call-done = (f32[3,3,128,64]{2,3,1,0:T(8,128)}, f32[3,3,128,256]{2,3,1,0:T(8,128)}) async-done(((f32[3,3,128,64]{2,3,1,0:T(8,128)}, f32[3,3,128,256]{2,3,1,0:T(8,128)}), (f32[3,3,128,64]{2,3,1,0:T(8,128)}, f32[3,3,128,256]{2,3,1,0:T(8,128)})) %all-reduce.6.cloned.1.call-update) | async-done | bytes 1474576 | tf_op jit(solution)/shard_map/psum | solution.py:159
  479.6 1.7 broadcast_multiply_fusion.1
  (223 shorter events, 59.2 us)
Async XLA Ops:
  7.2 79.8 %copy-start = (s32[4096]{0:T(1024)S(1)}, s32[4096]{0:T(1024)}, u32[]{:S(2)}) copy-start(s32[4096]{0:T(1024)} %param.13) | copy-start | bytes 49156
  7.2 20.8 %copy-start.2 = (bf16[4096]{0:T(1024)(128)(2,1)S(1)}, bf16[4096]{0:T(1024)(128)(2,1)}, u32[]{:S(2)}) copy-start(bf16[4096]{0:T(1024)(128)(2,1)} %param.11) | copy-start | bytes 24580
  80.7 52.5 %all-to-all-start.2 = ((bf16[8,2,512]{2,1,0:T(2,128)(2,1)}), bf16[8,2,512]{2,1,0:T(2,128)(2,1)S(1)}, u32[]{:S(2)}, u32[]{:S(2)}) async-start(bf16[8,2,512]{2,1,0:T(2,128)(2,1)} %reshape.179), calls=%async_computation.2 | async-start | bytes 32768 | tf_op jit(solution)/shard_map/all_to_all | solution.py:132
  87.0 51.3 %copy-start.19 = (bf16[3,3,128,256]{3,2,1,0:T(8,128)(2,1)S(1)}, bf16[3,3,128,256]{3,2,1,0:T(8,128)(2,1)}, u32[]{:S(2)}) copy-start(bf16[3,3,128,256]{3,2,1,0:T(8,128)(2,1)} %param.15) | copy-start | bytes 1769476
  133.2 41.7 %all-to-all-start.1 = ((s32[8,1,1024]{2,1,0:T(1,128)}), s32[8,1,1024]{2,1,0:T(1,128)S(1)}, u32[]{:S(2)}, u32[]{:S(2)}) async-start(s32[8,1,1024]{2,1,0:T(1,128)} %bitcast.2), calls=%async_computation.1 | async-start | bytes 65536 | tf_op jit(solution)/shard_map/all_to_all | solution.py:133
  144.2 4.6 copy-start.28
  174.8 4.5 copy-start.17
  174.9 4.5 copy-start.18
  174.9 16.3 %all-to-all-start.3 = ((bf16[3,3,128,256]{2,1,0,3:T(4,128)(2,1)}), bf16[3,3,128,256]{2,1,0,3:T(4,128)(2,1)}, u32[]{:S(2)}, u32[]{:S(2)}) async-start(bf16[3,3,128,256]{2,1,0,3:T(4,128)(2,1)} %copy.125), calls=%async_computation.3 | async-start | bytes 1572864 | tf_op jit(solution)/shard_map/all_to_all | solution.py:153
  182.9 13.1 %copy-start.25 = (bf16[128,8,384]{2,1,0:T(8,128)(2,1)S(1)}, bf16[128,8,384]{2,1,0:T(8,128)(2,1)}, u32[]{:S(2)}) copy-start(bf16[128,8,384]{2,1,0:T(8,128)(2,1)} %param.17) | copy-start | bytes 2359300
  191.2 33.3 %all-to-all-start = ((bf16[8,2,32768]{2,1,0:T(2,128)(2,1)}), bf16[8,2,32768]{2,1,0:T(2,128)(2,1)S(1)}, u32[]{:S(2)}, u32[]{:S(2)}) async-start(bf16[8,2,32768]{2,1,0:T(2,128)(2,1)} %reshape.177), calls=%async_computation | async-start | bytes 2097152 | tf_op jit(solution)/shard_map/all_to_all | solution.py:131
  195.9 86.4 %all-gather.5.cloned.1.call-start = ((), (), s32[]{:S(2)}) async-start(), calls=%async_computation.6 | async-start | bytes 3010560 | tf_op jit(solution)/shard_map/all_gather | solution.py:152
  196.5 25.7 %copy-start.10 = (bf16[128,8,384]{0,2,1:T(8,128)(2,1)}, bf16[128,8,384]{0,2,1:T(8,128)(2,1)S(1)}, u32[]{:S(2)}) copy-start(bf16[128,8,384]{0,2,1:T(8,128)(2,1)S(1)} %copy.122) | copy-start | bytes 2359300
  196.6 19.5 %collective-permute-start.8 = (bf16[128,1,384]{0,2,1:T(8,128)(2,1)S(1)}, bf16[128,1,384]{0,2,1:T(8,128)(2,1)S(1)}, u32[]{:S(2)}, u32[]{:S(2)}) collective-permute-start(bf16[128,1,384]{0,2,1:T(8,128)(2,1)S(1)} %get-tuple-element.104), channel_id=1, source_target_pairs={{0,4},{4,8},{8,12},{1,5},{5,9},{9,13},{2,6},{6,10},{10,14},{3,7},{... | collective-permute-start | bytes 294920 | tf_op jit(solution)/shard_map/ppermute | solution.py:13
  200.4 15.6 %collective-permute-start.9 = (bf16[128,1,384]{0,2,1:T(8,128)(2,1)S(1)}, bf16[128,1,384]{0,2,1:T(8,128)(2,1)S(1)}, u32[]{:S(2)}, u32[]{:S(2)}) collective-permute-start(bf16[128,1,384]{0,2,1:T(8,128)(2,1)S(1)} %get-tuple-element.105), channel_id=1, source_target_pairs={{4,0},{8,4},{12,8},{5,1},{9,5},{13,9},{6,2},{10,6},{14,10},{7,3},{... | collective-permute-start | bytes 294920 | tf_op jit(solution)/shard_map/ppermute | solution.py:16
  216.0 3.2 collective-permute-start.10
  217.9 3.1 collective-permute-start.11
  222.2 101.3 %all-reduce.4.cloned.1.call-start = ((), (), s32[]{:S(2)}) async-start(), calls=%async_computation.4 | async-start | bytes 1572864 | tf_op jit(solution)/shard_map/psum | solution.py:141
  234.1 1.7 copy-start.26
  238.1 0.9 copy-start.27
  239.0 1.7 copy-start.26
  242.9 0.9 copy-start.27
  243.9 1.7 copy-start.26
  247.8 0.9 copy-start.27
  248.7 1.7 copy-start.26
  252.7 0.9 copy-start.27
  253.6 1.7 copy-start.26
  257.5 0.9 copy-start.27
  258.5 1.8 copy-start.26
  262.4 0.9 copy-start.27
  263.3 1.7 copy-start.26
  267.3 0.9 copy-start.27
  268.2 1.7 copy-start.26
  272.1 0.9 copy-start.27
  273.0 9.3 %copy-start.21 = (bf16[3,3,128,2,128]{4,2,3,1,0:T(8,128)(2,1)S(1)}, bf16[3,3,128,2,128]{4,2,3,1,0:T(8,128)(2,1)}, u32[]{:S(2)}) copy-start(bf16[3,3,128,2,128]{4,2,3,1,0:T(8,128)(2,1)} %copy.126) | copy-start | bytes 1769476
  282.0 127.7 %all-gather.3.cloned.1.call-start = ((), (), s32[]{:S(2)}) async-start(), calls=%async_computation.5 | async-start | bytes 3010560 | tf_op jit(solution)/shard_map/all_gather | solution.py:148
  282.3 3.3 copy-start.4
  296.2 33.2 %copy-start.29 = (bf16[3,3,128,64]{2,3,1,0:T(8,128)(2,1)S(1)}, bf16[3,3,128,64]{2,3,1,0:T(8,128)(2,1)}, u32[]{:S(2)}) copy-start(bf16[3,3,128,64]{2,3,1,0:T(8,128)(2,1)} %param.14) | copy-start | bytes 442372
  324.7 5.1 %collective-permute-start = (bf16[64,1,384]{2,0,1:T(8,128)(2,1)S(1)}, bf16[64,1,384]{2,0,1:T(8,128)(2,1)S(1)}, u32[]{:S(2)}, u32[]{:S(2)}) collective-permute-start(bf16[64,1,384]{2,0,1:T(8,128)(2,1)S(1)} %get-tuple-element.112), channel_id=1, source_target_pairs={{0,4},{4,8},{8,12},{1,5},{5,9},{9,13},{2,6},{6,10},{10,14},{3,7},{... | collective-permute-start | bytes 147464 | tf_op jit(solution)/shard_map/ppermute | solution.py:13
  328.1 6.0 %collective-permute-start.1 = (bf16[64,1,384]{2,0,1:T(8,128)(2,1)S(1)}, bf16[64,1,384]{2,0,1:T(8,128)(2,1)S(1)}, u32[]{:S(2)}, u32[]{:S(2)}) collective-permute-start(bf16[64,1,384]{2,0,1:T(8,128)(2,1)S(1)} %get-tuple-element.113), channel_id=1, source_target_pairs={{4,0},{8,4},{12,8},{5,1},{9,5},{13,9},{6,2},{10,6},{14,10},{7,3},{... | collective-permute-start | bytes 147464 | tf_op jit(solution)/shard_map/ppermute | solution.py:16
  334.2 5.2 %collective-permute-start.3 = (bf16[64,10,1]{2,0,1:T(8,128)(2,1)S(1)}, bf16[64,10,1]{2,0,1:T(8,128)(2,1)S(1)}, u32[]{:S(2)}, u32[]{:S(2)}) collective-permute-start(bf16[64,10,1]{2,0,1:T(8,128)(2,1)S(1)} %get-tuple-element.110), channel_id=1, source_target_pairs={{1,0},{3,2},{5,4},{7,6},{9,8},{11,10},{13,12},{15,14},{17,16},{19,... | collective-permute-start | bytes 3848 | tf_op jit(solution)/shard_map/ppermute | solution.py:16
  335.5 4.1 collective-permute-start.2
  340.0 9.8 %copy-start.5 = (bf16[64,10,385]{2,0,1:T(8,128)(2,1)}, bf16[64,10,385]{2,0,1:T(8,128)(2,1)S(1)}, u32[]{:S(2)}) copy-start(bf16[64,10,385]{2,0,1:T(8,128)(2,1)S(1)} %get-tuple-element.109) | copy-start | bytes 1478404
  340.0 10.1 %copy-start.7 = (bf16[64,10,385]{2,0,1:T(8,128)(2,1)}, bf16[64,10,385]{2,0,1:T(8,128)(2,1)S(1)}, u32[]{:S(2)}) copy-start(bf16[64,10,385]{2,0,1:T(8,128)(2,1)S(1)} %get-tuple-element.108) | copy-start | bytes 1478404
  342.4 1.6 copy-start.12
  342.4 1.9 copy-start.13
  342.4 2.3 copy-start.14
  342.4 3.1 copy-start.15
  342.4 3.5 copy-start.16
  342.4 4.0 copy-start.22
  342.5 4.4 copy-start.23
  342.5 4.9 copy-start.24
  344.0 16.6 %copy-start.9 = (bf16[128,8,384]{0,2,1:T(8,128)(2,1)}, bf16[128,8,384]{0,2,1:T(8,128)(2,1)S(1)}, u32[]{:S(2)}) copy-start(bf16[128,8,384]{0,2,1:T(8,128)(2,1)S(1)} %get-tuple-element.116) | copy-start | bytes 2359300
  350.4 6.0 %collective-permute-start.4 = (bf16[128,1,384]{0,2,1:T(8,128)(2,1)S(1)}, bf16[128,1,384]{0,2,1:T(8,128)(2,1)S(1)}, u32[]{:S(2)}, u32[]{:S(2)}) collective-permute-start(bf16[128,1,384]{0,2,1:T(8,128)(2,1)S(1)} %get-tuple-element.106), channel_id=1, source_target_pairs={{0,4},{4,8},{8,12},{1,5},{5,9},{9,13},{2,6},{6,10},{10,14},{3,7},{... | collective-permute-start | bytes 294920 | tf_op jit(solution)/shard_map/ppermute | solution.py:13
  353.9 6.7 %collective-permute-start.5 = (bf16[128,1,384]{0,2,1:T(8,128)(2,1)S(1)}, bf16[128,1,384]{0,2,1:T(8,128)(2,1)S(1)}, u32[]{:S(2)}, u32[]{:S(2)}) collective-permute-start(bf16[128,1,384]{0,2,1:T(8,128)(2,1)S(1)} %get-tuple-element.107), channel_id=1, source_target_pairs={{4,0},{8,4},{12,8},{5,1},{9,5},{13,9},{6,2},{10,6},{14,10},{7,3},{... | collective-permute-start | bytes 294920 | tf_op jit(solution)/shard_map/ppermute | solution.py:16
  360.5 17.3 %collective-permute-start.6 = (bf16[128,10,1]{0,2,1:T(2,128)(2,1)S(1)}, bf16[128,10,1]{0,2,1:T(2,128)(2,1)S(1)}, u32[]{:S(2)}, u32[]{:S(2)}) collective-permute-start(bf16[128,10,1]{0,2,1:T(2,128)(2,1)S(1)} %get-tuple-element.102), channel_id=1, source_target_pairs={{0,1},{2,3},{4,5},{6,7},{8,9},{10,11},{12,13},{14,15},{16,17},{18,... | collective-permute-start | bytes 7688 | tf_op jit(solution)/shard_map/ppermute | solution.py:13
  361.8 16.0 %collective-permute-start.7 = (bf16[128,10,1]{0,2,1:T(2,128)(2,1)S(1)}, bf16[128,10,1]{0,2,1:T(2,128)(2,1)S(1)}, u32[]{:S(2)}, u32[]{:S(2)}) collective-permute-start(bf16[128,10,1]{0,2,1:T(2,128)(2,1)S(1)} %get-tuple-element.103), channel_id=1, source_target_pairs={{1,0},{3,2},{5,4},{7,6},{9,8},{11,10},{13,12},{15,14},{17,16},{19,... | collective-permute-start | bytes 7688 | tf_op jit(solution)/shard_map/ppermute | solution.py:16
  380.2 1.1 copy-start.6
  380.3 1.3 copy-start.8
  380.3 99.4 %all-reduce.6.cloned.1.call-start = ((), (), s32[]{:S(2)}) async-start(), calls=%async_computation.7 | async-start | bytes 2949120 | tf_op jit(solution)/shard_map/psum | solution.py:159
  383.3 28.8 %copy-start.11 = (bf16[128,8,384]{0,2,1:T(8,128)(2,1)S(1)}, bf16[128,8,384]{0,2,1:T(8,128)(2,1)}, u32[]{:S(2)}) copy-start(bf16[128,8,384]{0,2,1:T(8,128)(2,1)} %copy-done.10) | copy-start | bytes 2359300
  409.7 2.4 copy-start.3
  417.3 1.2 copy-start.20
  481.3 2.8 copy-start.1
  (1 other events, 0.8 us)
Sparse Core Ops, SparseCore 0:
  222.3 37.8 all-gather.4
  282.2 41.2 all-reduce.3
  380.4 29.2 all-gather.2
  418.6 61.0 all-reduce.5
where the time goes:
time: 501 us; the launch traced here: 491 us
  local copies, waits for them, and re-layouts  174 us (35%)
  waiting for transfers between devices  139 us (28%)
  matrix products  69.9 us (14%)
  starting transfers between devices  46 us (9%)
  other arithmetic  25.3 us (5%)
  blocking collectives  21.6 us (4%)
  between operations  15.1 us (3%)
    psum x1, waiting for transfers between devices, body(): lax.psum((grad_one, grad_two, grad_gain), ('tile', 'sub'))  54.1 us
    gather x1, local copies, waits for them, and re-layouts, body(): jnp.take(obs_weight, pick)  50.7 us
    gather x1, local copies, waits for them, and re-layouts, body(): jnp.take(obs_cell, pick)  45.5 us
    all_gather x1, waiting for transfers between devices, body(): hidden_pad = lax.all_gather(hidden_own, 'chan', axis=0, tiled=True)  25.9 us
    gather x2, local copies, waits for them, and re-layouts, body(): jnp.take(obs_values, pick, axis=0)  25.6 us
    psum x1, waiting for transfers between devices, body(): data_sum, density = lax.psum((data_part, dens_part), 'chan')  25.5 us
    dot_general x9, matrix products, back_apply(): jnp.einsum('oc,ohw->chw', kernel_cols[row_off, col_off], window, preferre...  18.1 us
    dot_general x8, matrix products, add_block(): jnp.einsum('ij,ci->jc', block_vals, placing, preferred_element_type=jnp.f...  17.4 us
  transfers between devices with their start and end apart: 20, of which 10 were waited for; matrix products, arithmetic and copies ran while one was open for 33% of the time, Pallas kernels for 0%

commit v1 on v0

--- a/solution.py
+++ b/solution.py
@@ -156,7 +156,9 @@
     grad_pre = (grad_hidden * sigma * (1.0 + pre_one * (1.0 - sigma))).astype(jnp.bfloat16)
     grad_one = kernel_grad(grad_pre, feats_pad)
     grad_gain = jnp.sum(grad_pre.astype(jnp.float32) * log_density[None], axis=(1, 2))
-    summed_one, summed_two, summed_gain = lax.psum((grad_one, grad_two, grad_gain), ("tile", "sub"))
+    summed_one, summed_two, summed_gain = lax.psum(
+        lax.psum((grad_one, grad_two, grad_gain), "sub"), "tile"
+    )
     scale_factor = 1.0 / math.sqrt(n_tiles * n_cells)
     return (
         encoded,

time: 501 us -> 535 us (1.068)
  waiting for transfers between devices: 139 us -> 161 us
  matrix products: 69.9 us -> 89.5 us
  local copies, waits for them, and re-layouts: 174 us -> 168 us
    psum x1 -> x2, waiting for transfers between devices: 54.1 us -> 75.3 us  [the longest x1 64 us: body(): lax.psum(lax.psum((grad_one, grad_two, grad_gain), 'sub'), 'tile')]
    dot_general x8, matrix products: 17.4 us -> 31.4 us  [add_block(): jnp.einsum('ij,ci->jc', block_vals, placing, preferred_element_type=jnp.f...]
    while x32 -> x0, local copies, waits for them, and re-layouts: 7.04 us -> none
    dot_general x18, matrix products: 10.6 us -> 16.5 us  [conv_apply(): jnp.einsum('oc,chw->ohw', kernel[row_off, col_off], window, preferred_ele...]
    unnamed x69 -> x79, local copies, waits for them, and re-layouts: 12.4 us -> 14.1 us
    psum x1 -> x2, blocking collectives: 14.7 us -> 13.1 us  [the longest x1 9.81 us: body(): lax.psum(lax.psum((grad_one, grad_two, grad_gain), 'sub'), 'tile')]
  transfers between devices with their start and end apart: 20 -> 21, of which waited for: 10 -> 11; matrix products, arithmetic and copies ran while one was open for 33% -> 34% of each run, Pallas kernels for 0% -> 0%
where the time goes in v1:
time: 535 us; the launch traced here: 525 us
  local copies, waits for them, and re-layouts  168 us (31%)
  waiting for transfers between devices  161 us (30%)
  matrix products  89.5 us (17%)
  starting transfers between devices  46.1 us (9%)
  other arithmetic  25.3 us (5%)
  blocking collectives  20.3 us (4%)
  between operations  15.2 us (3%)
    psum x1, waiting for transfers between devices, body(): lax.psum(lax.psum((grad_one, grad_two, grad_gain), 'sub'), 'tile')  64 us
    gather x1, local copies, waits for them, and re-layouts, body(): jnp.take(obs_weight, pick)  50.7 us
    gather x1, local copies, waits for them, and re-layouts, body(): jnp.take(obs_cell, pick)  45.5 us
    dot_general x8, matrix products, add_block(): jnp.einsum('ij,ci->jc', block_vals, placing, preferred_element_type=jnp.f...  31.4 us
    all_gather x1, waiting for transfers between devices, body(): hidden_pad = lax.all_gather(hidden_own, 'chan', axis=0, tiled=True)  25.9 us
    psum x1, waiting for transfers between devices, body(): data_sum, density = lax.psum((data_part, dens_part), 'chan')  25.7 us
    gather x2, local copies, waits for them, and re-layouts, body(): jnp.take(obs_values, pick, axis=0)  25.6 us
    dot_general x9, matrix products, back_apply(): jnp.einsum('oc,ohw->chw', kernel_cols[row_off, col_off], window, preferre...  18.1 us
  transfers between devices with their start and end apart: 21, of which 11 were waited for; matrix products, arithmetic and copies ran while one was open for 34% of the time, Pallas kernels for 0%

profile of v1, /device:TPU:0, one launch (start us, length us, event | category | flops | bytes accessed | tf_op | source)
XLA Modules:
  0.0 525.5 jit_solution(8213744835553815645)
XLA Ops:
  7.9 2.3 reduce-window.6
  12.4 15.5 %scatter_custom_fusion = s32[8192]{0:T(1024)S(1)} fusion(s32[4096]{0:T(1024)S(1)} %compare_select_fusion.1, s32[4096]{0:T(1024)S(1)} %iota.14, s32[]{:T(128)} %constant.46.clone.1), kind=kCustom, calls=%fused_computation.211 | custom fusion | bytes 32772 | tf_op jit(solution)/shard_map/scatter | solution.py:118
  28.0 50.7 %gather_fusion.2 = bf16[8192]{0:T(1024)(128)(2,1)S(1)} fusion(bf16[4096]{0:T(1024)(128)(2,1)S(1)} %copy-done.2, s32[8192]{0:T(1024)S(1)} %fusion.153), kind=kCustom, calls=%fused_computation.2 | custom fusion | bytes 65536 | tf_op jit(solution)/shard_map/jit(_take)/gather | solution.py:127
  80.7 6.3 %all-to-all-start.2 = ((bf16[8,2,512]{2,1,0:T(2,128)(2,1)}), bf16[8,2,512]{2,1,0:T(2,128)(2,1)S(1)}, u32[]{:S(2)}, u32[]{:S(2)}) async-start(bf16[8,2,512]{2,1,0:T(2,128)(2,1)} %reshape.179), calls=%async_computation.2 | async-start | bytes 32768 | tf_op jit(solution)/shard_map/all_to_all | solution.py:132
  87.0 45.5 %gather_fusion.1 = s32[8192]{0:T(1024)S(1)} fusion(s32[4096]{0:T(1024)S(1)} %copy-done, s32[8192]{0:T(1024)S(1)} %fusion.153), kind=kCustom, calls=%fused_computation.1 | custom fusion | bytes 98304 | tf_op jit(solution)/shard_map/jit(_take)/gather | solution.py:129
  133.2 5.1 all-to-all-start.1
  139.6 2.1 broadcast_in_dim.90
  141.7 2.5 broadcast_in_dim.91
  144.2 2.1 broadcast_in_dim.93
  146.3 2.5 broadcast_in_dim.94
  149.3 24.0 %gather_fusion = bf16[8192,64]{1,0:T(8,128)(2,1)S(1)} fusion(bf16[4096,64]{1,0:T(8,128)(2,1)S(1)} %copy.118, s32[8192]{0:T(1024)S(1)} %fusion.153), kind=kCustom, calls=%fused_computation | custom fusion | bytes 2129920 | tf_op jit(solution)/shard_map/jit(_take)/gather | solution.py:123
  174.9 4.5 all-to-all-start.3
  181.0 1.9 reshape.177
  182.9 8.3 %all-to-all-done.3 = bf16[3,3,128,256]{2,1,0,3:T(4,128)(2,1)} async-done(((bf16[3,3,128,256]{2,1,0,3:T(4,128)(2,1)}), bf16[3,3,128,256]{2,1,0,3:T(4,128)(2,1)}, u32[]{:S(2)}, u32[]{:S(2)}) %all-to-all-start.3) | async-done | bytes 589856 | tf_op jit(solution)/shard_map/all_to_all | solution.py:153
  191.2 4.7 all-to-all-start
  196.6 3.9 collective-permute-start.8
  201.9 14.1 %collective-permute-done.8 = bf16[128,1,384]{0,2,1:T(8,128)(2,1)S(1)} collective-permute-done((bf16[128,1,384]{0,2,1:T(8,128)(2,1)S(1)}, bf16[128,1,384]{0,2,1:T(8,128)(2,1)S(1)}, u32[]{:S(2)}, u32[]{:S(2)}) %collective-permute-start.8) | collective-permute-done | bytes 98336 | tf_op jit(solution)/shard_map/ppermute | solution.py:13
  216.0 1.8 collective-permute-start.10
  222.3 2.2 copy.126
  225.5 6.4 %reduce.2 = bf16[8,65536]{1,0:T(8,128)(2,1)S(1)} reduce(bf16[8,1,65536]{2,1,0:T(2,128)(2,1)S(1)} %reshape.178, bf16[]{:T(256)} %constant.88), dimensions={1}, to_apply=%all_to_all.33.reduce_sub_computation | reduce | bytes 2097154 | tf_op jit(solution)/shard_map/all_to_all | solution.py:131
  231.9 2.2 reshape_reshape.3
  234.1 45.6 %while.13 = (s32[]{:T(128)}, f32[64,3072]{1,0:T(8,128)}, f32[3072]{0:T(1024)S(1)}, bf16[8,1024,64]{2,1,0:T(8,128)(2,1)S(1)}, s32[8,1024]{1,0:T(8,128)S(1)}, /*in...) while((s32[]{:T(128)}, f32[64,3072]{1,0:T(8,128)}, f32[3072]{0:T(1024)S(1)}, ...), condition=%wide.region_5.6_spmd.clone, body=%wide.region_4.5_spmd.clone.sunk | while | flops 421926912 | bytes 1908852 | solution.py:92
  234.2 1.7 fusion.214
  235.9 2.9 fusion.213
  238.9 1.7 fusion.214
  240.6 4.1 fusion.213
  244.7 1.7 fusion.214
  246.5 4.1 fusion.213
  250.6 1.7 fusion.214
  252.3 4.1 fusion.213
  256.4 1.7 fusion.214
  258.1 4.1 fusion.213
  262.2 1.7 fusion.214
  264.0 4.1 fusion.213
  269.8 4.1 fusion.213
  273.9 1.7 fusion.214
  275.6 4.1 fusion.213
  279.7 2.1 copy.182
  281.8 7.2 %psum.57 = f32[8,384]{1,0:T(8,128)S(1)} all-reduce(f32[8,384]{1,0:T(8,128)S(1)} %reshape.88), channel_id=1, replica_groups=mesh['member'=2,'tile'=4,'chan'=2,'sub'=2] {'chan'}, use_global_device_ids=true, to_apply=%region_7.8 | all-reduce | flops 3072 | bytes 24576 | tf_op jit(solution)/shard_map/psum | solution.py:141
  289.2 3.3 fusion.25
  292.5 1.8 fusion.27
  294.2 1.7 fusion.29
  296.0 1.8 fusion.31
  297.8 1.7 fusion.33
  301.2 1.8 fusion.37
  303.0 1.8 fusion.39
  304.8 25.7 %all-reduce.6.cloned.1.call-done = f32[64,8,384]{2,0,1:T(8,128)} async-done(((f32[64,8,384]{2,0,1:T(8,128)}), f32[64,8,384]{2,0,1:T(8,128)}) %all-reduce.6.cloned.1.call-update) | async-done | bytes 786448 | tf_op jit(solution)/shard_map/psum | solution.py:141
  331.7 3.4 collective-permute-start
  336.9 4.3 collective-permute-done.1
  342.5 3.0 collective-permute-start.2
  354.3 2.4 multiply_reduce_fusion
  357.4 3.4 collective-permute-start.4
  363.4 4.1 collective-permute-done.5
  370.2 3.3 psum.62
  373.4 9.8 %psum.63 = f32[128]{0:T(128)S(1)} all-reduce(f32[128]{0:T(128)S(1)} %psum.62), channel_id=1, replica_groups=mesh['member'=2,'tile'=4,'chan'=2,'sub'=2] {'tile'}, use_global_device_ids=true, to_apply=%region_14.15 | all-reduce | flops 128 | bytes 1024 | tf_op jit(solution)/shard_map/psum | solution.py:159
  383.2 2.4 pad_maximum_fusion.1
  389.2 25.9 %all-gather.3.cloned.1.call-done = bf16[256,10,386]{0,2,1:T(8,128)(2,1)} async-done(((bf16[128,10,386]{0,2,1:T(8,128)(2,1)}), bf16[256,10,386]{0,2,1:T(8,128)(2,1)}) %all-gather.3.cloned.1.call-update) | async-done | bytes 1976336 | tf_op jit(solution)/shard_map/all_gather | solution.py:148
  415.1 2.2 fusion.101
  424.0 1.8 fusion.50
  427.5 1.7 fusion.58
  429.2 1.8 fusion.62
  431.0 1.7 fusion.66
  432.7 11.4 %all-reduce.10.cloned.1.call-done = (f32[3,3,128,64]{2,3,1,0:T(8,128)}, f32[3,3,128,256]{2,3,1,0:T(8,128)}) async-done(((f32[3,3,128,64]{2,3,1,0:T(8,128)}, f32[3,3,128,256]{2,3,1,0:T(8,128)}), (f32[3,3,128,64]{2,3,1,0:T(8,128)}, f32[3,3,128,256]{2,3,1,0:T(8,128)})) %all-reduce.10.cloned.1.call-update) | async-done | bytes 1474576 | tf_op jit(solution)/shard_map/psum | solution.py:160
  450.0 64.0 %all-reduce.8.cloned.1.call-done = (f32[3,3,128,64]{2,3,1,0:T(8,128)}, f32[3,3,128,256]{2,3,1,0:T(8,128)}) async-done(((f32[3,3,128,64]{2,3,1,0:T(8,128)}, f32[3,3,128,256]{2,3,1,0:T(8,128)}), (f32[3,3,128,64]{2,3,1,0:T(8,128)}, f32[3,3,128,256]{2,3,1,0:T(8,128)})) %all-reduce.8.cloned.1.call-update) | async-done | bytes 1474576 | tf_op jit(solution)/shard_map/psum | solution.py:159
  (205 shorter events, 62.6 us)
Async XLA Ops:
  7.2 79.8 %copy-start = (s32[4096]{0:T(1024)S(1)}, s32[4096]{0:T(1024)}, u32[]{:S(2)}) copy-start(s32[4096]{0:T(1024)} %param.13) | copy-start | bytes 49156
  7.2 20.8 %copy-start.2 = (bf16[4096]{0:T(1024)(128)(2,1)S(1)}, bf16[4096]{0:T(1024)(128)(2,1)}, u32[]{:S(2)}) copy-start(bf16[4096]{0:T(1024)(128)(2,1)} %param.11) | copy-start | bytes 24580
  80.7 52.5 %all-to-all-start.2 = ((bf16[8,2,512]{2,1,0:T(2,128)(2,1)}), bf16[8,2,512]{2,1,0:T(2,128)(2,1)S(1)}, u32[]{:S(2)}, u32[]{:S(2)}) async-start(bf16[8,2,512]{2,1,0:T(2,128)(2,1)} %reshape.179), calls=%async_computation.2 | async-start | bytes 32768 | tf_op jit(solution)/shard_map/all_to_all | solution.py:132
  87.0 51.3 %copy-start.23 = (bf16[3,3,128,256]{3,2,1,0:T(8,128)(2,1)S(1)}, bf16[3,3,128,256]{3,2,1,0:T(8,128)(2,1)}, u32[]{:S(2)}) copy-start(bf16[3,3,128,256]{3,2,1,0:T(8,128)(2,1)} %param.15) | copy-start | bytes 1769476
  133.2 41.7 %all-to-all-start.1 = ((s32[8,1,1024]{2,1,0:T(1,128)}), s32[8,1,1024]{2,1,0:T(1,128)S(1)}, u32[]{:S(2)}, u32[]{:S(2)}) async-start(s32[8,1,1024]{2,1,0:T(1,128)} %bitcast.2), calls=%async_computation.1 | async-start | bytes 65536 | tf_op jit(solution)/shard_map/all_to_all | solution.py:133
  144.2 4.6 copy-start.31
  174.9 4.5 copy-start.21
  174.9 4.5 copy-start.22
  174.9 16.3 %all-to-all-start.3 = ((bf16[3,3,128,256]{2,1,0,3:T(4,128)(2,1)}), bf16[3,3,128,256]{2,1,0,3:T(4,128)(2,1)}, u32[]{:S(2)}, u32[]{:S(2)}) async-start(bf16[3,3,128,256]{2,1,0,3:T(4,128)(2,1)} %copy.125), calls=%async_computation.3 | async-start | bytes 1572864 | tf_op jit(solution)/shard_map/all_to_all | solution.py:153
  182.9 13.1 %copy-start.30 = (bf16[128,8,384]{2,1,0:T(8,128)(2,1)S(1)}, bf16[128,8,384]{2,1,0:T(8,128)(2,1)}, u32[]{:S(2)}) copy-start(bf16[128,8,384]{2,1,0:T(8,128)(2,1)} %param.17) | copy-start | bytes 2359300
  191.2 33.3 %all-to-all-start = ((bf16[8,2,32768]{2,1,0:T(2,128)(2,1)}), bf16[8,2,32768]{2,1,0:T(2,128)(2,1)S(1)}, u32[]{:S(2)}, u32[]{:S(2)}) async-start(bf16[8,2,32768]{2,1,0:T(2,128)(2,1)} %reshape.177), calls=%async_computation | async-start | bytes 2097152 | tf_op jit(solution)/shard_map/all_to_all | solution.py:131
  195.9 93.2 %all-gather.5.cloned.1.call-start = ((), (), s32[]{:S(2)}) async-start(), calls=%async_computation.6 | async-start | bytes 3010560 | tf_op jit(solution)/shard_map/all_gather | solution.py:152
  196.5 25.7 %copy-start.10 = (bf16[128,8,384]{0,2,1:T(8,128)(2,1)}, bf16[128,8,384]{0,2,1:T(8,128)(2,1)S(1)}, u32[]{:S(2)}) copy-start(bf16[128,8,384]{0,2,1:T(8,128)(2,1)S(1)} %copy.122) | copy-start | bytes 2359300
  196.6 19.5 %collective-permute-start.8 = (bf16[128,1,384]{0,2,1:T(8,128)(2,1)S(1)}, bf16[128,1,384]{0,2,1:T(8,128)(2,1)S(1)}, u32[]{:S(2)}, u32[]{:S(2)}) collective-permute-start(bf16[128,1,384]{0,2,1:T(8,128)(2,1)S(1)} %get-tuple-element.106), channel_id=1, source_target_pairs={{0,4},{4,8},{8,12},{1,5},{5,9},{9,13},{2,6},{6,10},{10,14},{3,7},{... | collective-permute-start | bytes 294920 | tf_op jit(solution)/shard_map/ppermute | solution.py:13
  200.5 15.6 %collective-permute-start.9 = (bf16[128,1,384]{0,2,1:T(8,128)(2,1)S(1)}, bf16[128,1,384]{0,2,1:T(8,128)(2,1)S(1)}, u32[]{:S(2)}, u32[]{:S(2)}) collective-permute-start(bf16[128,1,384]{0,2,1:T(8,128)(2,1)S(1)} %get-tuple-element.107), channel_id=1, source_target_pairs={{4,0},{8,4},{12,8},{5,1},{9,5},{13,9},{6,2},{10,6},{14,10},{7,3},{... | collective-permute-start | bytes 294920 | tf_op jit(solution)/shard_map/ppermute | solution.py:16
  216.0 3.2 collective-permute-start.10
  217.9 3.1 collective-permute-start.11
  222.2 108.3 %all-reduce.6.cloned.1.call-start = ((), (), s32[]{:S(2)}) async-start(), calls=%async_computation.4 | async-start | bytes 1572864 | tf_op jit(solution)/shard_map/psum | solution.py:141
  279.7 9.4 %copy-start.25 = (bf16[3,3,128,2,128]{4,2,3,1,0:T(8,128)(2,1)S(1)}, bf16[3,3,128,2,128]{4,2,3,1,0:T(8,128)(2,1)}, u32[]{:S(2)}) copy-start(bf16[3,3,128,2,128]{4,2,3,1,0:T(8,128)(2,1)} %copy.126) | copy-start | bytes 1769476
  289.1 126.0 %all-gather.3.cloned.1.call-start = ((), (), s32[]{:S(2)}) async-start(), calls=%async_computation.5 | async-start | bytes 3010560 | tf_op jit(solution)/shard_map/all_gather | solution.py:148
  289.1 3.3 copy-start.4
  303.0 33.4 %copy-start.32 = (bf16[3,3,128,64]{2,3,1,0:T(8,128)(2,1)S(1)}, bf16[3,3,128,64]{2,3,1,0:T(8,128)(2,1)}, u32[]{:S(2)}) copy-start(bf16[3,3,128,64]{2,3,1,0:T(8,128)(2,1)} %param.14) | copy-start | bytes 442372
  331.7 5.1 collective-permute-start
  335.1 6.0 %collective-permute-start.1 = (bf16[64,1,384]{2,0,1:T(8,128)(2,1)S(1)}, bf16[64,1,384]{2,0,1:T(8,128)(2,1)S(1)}, u32[]{:S(2)}, u32[]{:S(2)}) collective-permute-start(bf16[64,1,384]{2,0,1:T(8,128)(2,1)S(1)} %get-tuple-element.115), channel_id=1, source_target_pairs={{4,0},{8,4},{12,8},{5,1},{9,5},{13,9},{6,2},{10,6},{14,10},{7,3},{... | collective-permute-start | bytes 147464 | tf_op jit(solution)/shard_map/ppermute | solution.py:16
  341.2 5.2 collective-permute-start.3
  342.5 4.1 collective-permute-start.2
  347.0 9.8 %copy-start.5 = (bf16[64,10,385]{2,0,1:T(8,128)(2,1)}, bf16[64,10,385]{2,0,1:T(8,128)(2,1)S(1)}, u32[]{:S(2)}) copy-start(bf16[64,10,385]{2,0,1:T(8,128)(2,1)S(1)} %get-tuple-element.111) | copy-start | bytes 1478404
  347.0 10.1 %copy-start.7 = (bf16[64,10,385]{2,0,1:T(8,128)(2,1)}, bf16[64,10,385]{2,0,1:T(8,128)(2,1)S(1)}, u32[]{:S(2)}) copy-start(bf16[64,10,385]{2,0,1:T(8,128)(2,1)S(1)} %get-tuple-element.110) | copy-start | bytes 1478404
  348.6 0.8 copy-start.33
  349.4 1.6 copy-start.12
  349.4 1.9 copy-start.13
  349.4 2.3 copy-start.14
  349.4 3.1 copy-start.15
  349.4 3.5 copy-start.16
  349.5 4.0 copy-start.26
  349.5 4.4 copy-start.27
  349.5 4.9 copy-start.28
  351.0 16.6 %copy-start.9 = (bf16[128,8,384]{0,2,1:T(8,128)(2,1)}, bf16[128,8,384]{0,2,1:T(8,128)(2,1)S(1)}, u32[]{:S(2)}) copy-start(bf16[128,8,384]{0,2,1:T(8,128)(2,1)S(1)} %get-tuple-element.118) | copy-start | bytes 2359300
  357.4 6.0 %collective-permute-start.4 = (bf16[128,1,384]{0,2,1:T(8,128)(2,1)S(1)}, bf16[128,1,384]{0,2,1:T(8,128)(2,1)S(1)}, u32[]{:S(2)}, u32[]{:S(2)}) collective-permute-start(bf16[128,1,384]{0,2,1:T(8,128)(2,1)S(1)} %get-tuple-element.108), channel_id=1, source_target_pairs={{0,4},{4,8},{8,12},{1,5},{5,9},{9,13},{2,6},{6,10},{10,14},{3,7},{... | collective-permute-start | bytes 294920 | tf_op jit(solution)/shard_map/ppermute | solution.py:13
  360.9 6.7 %collective-permute-start.5 = (bf16[128,1,384]{0,2,1:T(8,128)(2,1)S(1)}, bf16[128,1,384]{0,2,1:T(8,128)(2,1)S(1)}, u32[]{:S(2)}, u32[]{:S(2)}) collective-permute-start(bf16[128,1,384]{0,2,1:T(8,128)(2,1)S(1)} %get-tuple-element.109), channel_id=1, source_target_pairs={{4,0},{8,4},{12,8},{5,1},{9,5},{13,9},{6,2},{10,6},{14,10},{7,3},{... | collective-permute-start | bytes 294920 | tf_op jit(solution)/shard_map/ppermute | solution.py:16
  367.5 15.7 %collective-permute-start.6 = (bf16[128,10,1]{0,2,1:T(2,128)(2,1)S(1)}, bf16[128,10,1]{0,2,1:T(2,128)(2,1)S(1)}, u32[]{:S(2)}, u32[]{:S(2)}) collective-permute-start(bf16[128,10,1]{0,2,1:T(2,128)(2,1)S(1)} %get-tuple-element.104), channel_id=1, source_target_pairs={{0,1},{2,3},{4,5},{6,7},{8,9},{10,11},{12,13},{14,15},{16,17},{18,... | collective-permute-start | bytes 7688 | tf_op jit(solution)/shard_map/ppermute | solution.py:13
  368.8 14.4 %collective-permute-start.7 = (bf16[128,10,1]{0,2,1:T(2,128)(2,1)S(1)}, bf16[128,10,1]{0,2,1:T(2,128)(2,1)S(1)}, u32[]{:S(2)}, u32[]{:S(2)}) collective-permute-start(bf16[128,10,1]{0,2,1:T(2,128)(2,1)S(1)} %get-tuple-element.105), channel_id=1, source_target_pairs={{1,0},{3,2},{5,4},{7,6},{9,8},{11,10},{13,12},{15,14},{17,16},{19,... | collective-permute-start | bytes 7688 | tf_op jit(solution)/shard_map/ppermute | solution.py:16
  385.6 1.1 copy-start.6
  385.6 1.3 copy-start.8
  385.6 58.5 %all-reduce.10.cloned.1.call-start = ((), (), s32[]{:S(2)}) async-start(), calls=%async_computation.8 | async-start | bytes 2949120 | tf_op jit(solution)/shard_map/psum | solution.py:160
  387.3 27.8 %copy-start.11 = (bf16[128,8,384]{0,2,1:T(8,128)(2,1)S(1)}, bf16[128,8,384]{0,2,1:T(8,128)(2,1)}, u32[]{:S(2)}) copy-start(bf16[128,8,384]{0,2,1:T(8,128)(2,1)} %copy-done.10) | copy-start | bytes 2359300
  415.1 2.2 copy-start.3
  422.5 1.5 copy-start.24
  423.6 90.3 %all-reduce.8.cloned.1.call-start = ((), (), s32[]{:S(2)}) async-start(), calls=%async_computation.7 | async-start | bytes 2949120 | tf_op jit(solution)/shard_map/psum | solution.py:159
  444.1 1.8 copy-start.29
  444.7 1.5 copy-start.19
  444.7 2.0 copy-start.20
  445.3 1.9 copy-start.17
  445.3 2.4 copy-start.18
  515.7 2.8 copy-start.1
Sparse Core Ops, SparseCore 0:
  222.3 37.8 all-gather.4
  289.2 41.2 all-reduce.5
  385.7 29.2 all-gather.2
  423.7 20.3 all-reduce.9
  446.5 67.3 all-reduce.7
